TPU v7x, 32 devices: a whole 2x2x4 slice. The times are simulated.
32 devices in a mesh: clu: 8 (over z, x), grp: 4 (over y, core).
Axes of the slice: x: 2, y: 2, z: 4, core: 2. Of those that a mesh axis runs over, the one named last changes fastest.
Arguments:
- document_vectors: bfloat16 [8192, 768], P(('clu', 'grp')), may hold values from -100 to 100
- group_label: int32 [8192], P(('clu', 'grp')), may hold values from 0 to 7, as said below
- within_group_position: int32 [8192], P(('clu', 'grp')), may hold values from 0 to 8191, each once
- bucket_boundaries: int32 [128], replicated, may hold values from 0 to 1008, as said below
- threshold_smoothness: int32 [1], replicated, may hold values from 20 to 59
- desired_retention_share: int32 [1], replicated, may hold values from 300 to 700
Outputs:
- nearest: float32 [8192], P(('clu', 'grp'))
- keep_weight: float32 [8192], P(('clu', 'grp'))
Inputs may be any that keep to these rules, and one draw needn't show every extreme that they name: `group_label`: among the 256 documents of one device (aligned blocks of the encoder order) no cluster appears more than 64 times, and on every device exactly three clusters appear 64 times. `bucket_boundaries`: strictly increasing.
All inputs are finite; a program needn't handle non-finite values.
Results may differ from a plain program's by a relative error of at most 0.0003.
The roundings to bfloat16 on the way count: a program that leaves them out, or rounds other values in their place, can miss the bound.
Values may be sent and summed in bfloat16 or wider, within the bound.
No kernel may reach another device: no remote copies, remote signals or barrier semaphores. Data moves between devices by JAX's collectives and lax.ppermute only.
A program may use at most 64 MiB of HBM per device.

v0:
```python
import functools

import jax
import jax.numpy as jnp
from jax import lax
from jax.experimental import pallas as pl
from jax.experimental.pallas import tpu as pltpu
from jax.sharding import PartitionSpec as P

AXES = ("clu", "grp")
KEY_ROWS = 8


def vmem():
    return pl.BlockSpec(memory_space=pltpu.VMEM)


def flat_lanes(ref):
    return jnp.concatenate([ref[i : i + 1, :] for i in range(ref.shape[0])], axis=1)


def prep_kernel(rows_ref, label_ref, pos_ref, out_ref):
    docs, width = rows_ref.shape
    values = rows_ref[...].astype(jnp.float32)
    total = jnp.sum(values * values, axis=1, keepdims=True)
    out_ref[0:docs, :] = (values / jnp.sqrt(total + 1e-06)).astype(jnp.bfloat16)
    label = flat_lanes(label_ref)
    pos = flat_lanes(pos_ref)
    high = pos >> 8
    low = pos & 255
    key = jnp.concatenate([label, high, low], axis=1).astype(jnp.float32)
    rest = width - key.shape[1]
    if rest:
        key = jnp.concatenate([key, jnp.zeros((1, rest), jnp.float32)], axis=1)
    out_ref[docs:, :] = jnp.broadcast_to(key, (KEY_ROWS, width)).astype(jnp.bfloat16)


def keys_of(ref, docs, total_docs):
    key = ref[docs : docs + KEY_ROWS, :].astype(jnp.float32)
    start = key[:, 0:docs] * float(total_docs)
    return start + key[:, docs : 2 * docs] * 256.0 + key[:, 2 * docs : 3 * docs], start


def match_kernel(total_docs, docs, plans, has_start, *refs):
    out_ref = refs[-1]
    blocks = refs[1:-1] if has_start else refs[:-1]

    def run(plan):
        keys = {}

        def col_key(c):
            if c not in keys:
                key, _ = keys_of(blocks[c], docs, total_docs)
                keys[c] = jnp.transpose(key)[:, 0:1]
            return keys[c]

        for i, (r, cols) in enumerate(plan):
            best = refs[0][i : i + 1, :] if has_start else jnp.zeros((1, docs), jnp.float32)
            if cols:
                row = blocks[r]
                row_key, start = keys_of(row, docs, total_docs)
                row_key, start = row_key[0:1, :], start[0:1, :]
                for c in cols:
                    sims = lax.dot_general(
                        blocks[c][0:docs, :],
                        row[0:docs, :],
                        (((1,), (1,)), ((), ())),
                        preferred_element_type=jnp.float32,
                    )
                    key = col_key(c)
                    earlier = (key < row_key) & (key >= start)
                    best = jnp.maximum(
                        best, jnp.max(jnp.where(earlier, sims, 0.0), axis=0, keepdims=True)
                    )
            out_ref[i : i + 1, :] = best

    if len(plans) == 1:
        run(plans[0])
    else:
        core = lax.axis_index("grp") & 1
        for k, plan in enumerate(plans):
            pl.when(core == k)(functools.partial(run, plan))


def match(blocks, plans, docs, total_docs, start=None):
    width = blocks[0].shape[1]
    pairs = max(sum(len(cols) for _, cols in plan) for plan in plans)
    args = list(blocks) if start is None else [start] + list(blocks)
    return pl.pallas_call(
        functools.partial(match_kernel, total_docs, docs, plans, start is not None),
        out_shape=jax.ShapeDtypeStruct((len(plans[0]), docs), jnp.float32),
        in_specs=[vmem()] * len(args),
        out_specs=vmem(),
        cost_estimate=pl.CostEstimate(
            flops=2 * pairs * docs * docs * width,
            bytes_accessed=2 * docs * width * len(blocks),
            transcendentals=0,
        ),
        compiler_params=pltpu.CompilerParams(vmem_limit_bytes=24 << 20),
        name="match",
    )(*args)


def body(
    row_bits,
    col_bits,
    owners,
    group_size,
    document_vectors,
    group_label,
    within_group_position,
    bucket_boundaries,
    threshold_smoothness,
    desired_retention_share,
):
    docs, width = document_vectors.shape
    devices = owners * group_size
    total_docs = docs * devices
    bins = bucket_boundaries.shape[0]

    def send(value, pairs):
        return lax.ppermute(value, AXES, pairs)

    def swap(value, bit):
        return send(value, [(d, d ^ bit) for d in range(devices)])

    def split(value, even_bit, odd_bit):
        pairs = [(d, d ^ (odd_bit if d & 1 else even_bit)) for d in range(devices)]
        return send(value, pairs)

    own = pl.pallas_call(
        prep_kernel,
        out_shape=jax.ShapeDtypeStruct((docs + KEY_ROWS, width), jnp.bfloat16),
        in_specs=[vmem()] * 3,
        out_specs=vmem(),
        compiler_params=pltpu.CompilerParams(vmem_limit_bytes=24 << 20),
        name="prep",
    )(
        document_vectors,
        group_label.reshape(docs // 128, 128),
        within_group_position.reshape(docs // 128, 128),
    )
    if len(row_bits) == 2 and len(col_bits) == 3:
        far, y = row_bits
        z, x, _ = col_bits
        own_s = swap(own, 1)
        a1 = split(own, z, far)
        bx = swap(own, x)
        by = swap(own, y)
        a2 = split(own, far, z)
        bx_s = swap(bx, 1)
        f1 = split(a1, x, y)
        e1 = swap(a1, 1)
        g1 = swap(f1, 1)
        e2 = swap(a2, 1)
        f2 = split(a2, y, x)
        g2 = swap(f2, 1)
        row_masks = [0, y, far, y | far]
        near = match(
            [own, by, own_s, bx, bx_s],
            [[(0, [0, 2, 3, 4]), (1, [0, 2, 3, 4]), (0, []), (0, [])]],
            docs,
            total_docs,
        )
        blocks = [own, by, own_s, bx, bx_s, a1, f1, a2, e1, g1, e2]
        near = match(
            blocks,
            [
                [(0, [5, 6, 10]), (1, [5, 6, 10]), (7, [0, 2, 3, 4, 5, 6, 10]), (0, [])],
                [(0, [7, 8, 9]), (1, [7, 8, 9]), (5, [0, 2, 3, 4, 7, 8, 9]), (6, [0, 2, 3, 4, 7, 8, 9])],
            ],
            docs,
            total_docs,
            near,
        )
        blocks = [own, by, own_s, bx, bx_s, a1, f1, a2, f2, e2]
        near = match(
            blocks,
            [
                [(0, []), (0, []), (0, []), (8, [0, 2, 3, 4, 5, 6, 9])],
                [(0, [8]), (1, [8]), (5, [8]), (6, [8])],
            ],
            docs,
            total_docs,
            near,
        )
        near = match(
            [own, by, a2, f2, g2],
            [
                [(0, [4]), (1, [4]), (2, [4]), (3, [4])],
                [(0, []), (0, []), (0, []), (0, [])],
            ],
            docs,
            total_docs,
            near,
        )
    else:
        rows = {0: own}
        cols = {0: own}
        for bit in row_bits:
            rows.update({mask | bit: swap(block, bit) for mask, block in list(rows.items())})
        for bit in col_bits:
            cols.update({mask | bit: swap(block, bit) for mask, block in list(cols.items())})
        row_masks = sorted(rows)
        col_masks = sorted(cols)
        n = len(row_masks)
        blocks = [rows[m] for m in row_masks] + [cols[m] for m in col_masks]
        plan = [(i, list(range(n, len(blocks)))) for i in range(n)]
        near = match(blocks, [plan], docs, total_docs)
    near = near.reshape(len(row_masks), 1, docs)
    for bit in row_bits:
        other = swap(near, bit)
        index = [row_masks.index(m ^ bit) for m in row_masks]
        near = jnp.maximum(near, jnp.concatenate([other[i : i + 1] for i in index], axis=0))
    tau = threshold_smoothness[0].astype(jnp.float32) / 1000.0
    rate = desired_retention_share[0].astype(jnp.float32) / 1000.0
    edges = bucket_boundaries.astype(jnp.float32) / 1000.0
    above = jnp.sum(
        jax.nn.sigmoid((near.reshape(-1)[None, :] - edges[:, None]) / tau), axis=1
    ).reshape(1, bins)
    for bit in reversed(col_bits):
        above = above + swap(above, bit)
    below = 1.0 - above.reshape(bins) / total_docs
    cutoff = edges[0] + jnp.sum(
        (edges[1:] - edges[:-1]) * jax.nn.sigmoid((rate - below[:-1]) / 0.05)
    )
    nearest = near[0].reshape(docs)
    keep = jax.nn.sigmoid((cutoff - nearest) / tau)
    return nearest, keep


def solution(mesh):
    owners = mesh.shape["clu"]
    group_size = mesh.shape["grp"]
    core_bit = 1
    grp_bits = [1 << b for b in range(1, group_size.bit_length() - 1)]
    clu_bits = [group_size << b for b in range(owners.bit_length() - 1)]
    row_bits = [clu_bits[-1]] + grp_bits
    col_bits = [clu_bits[-2]] + clu_bits[:-2] + [core_bit]
    in_specs = (P(AXES, None), P(AXES), P(AXES), P(), P(), P())
    out_specs = (P(AXES), P(AXES))
    return jax.shard_map(
        functools.partial(body, row_bits, col_bits, owners, group_size),
        mesh=mesh,
        in_specs=in_specs,
        out_specs=out_specs,
        check_vma=False,
    )
```

profile of v0, /device:TPU:0, one launch (start us, length us, event | category | flops | bytes accessed | tf_op | source)
XLA Modules:
  0.0 59.9 jit_solution(9226615428134518344)
XLA Ops:
  0.6 0.0 copy-start.2
  0.6 0.0 copy-start.1
  0.6 0.7 %copy-done.2 = s32[256]{0:T(256)S(1)} copy-done((s32[256]{0:T(256)S(1)}, s32[256]{0:T(256)}, u32[]{:S(2)}) %copy-start.2) | copy-done | bytes 1048
  1.3 0.0 copy-done.1
  1.3 0.0 copy-start
  1.3 1.0 %copy-done = bf16[256,768]{1,0:T(8,128)(2,1)S(1)} copy-done((bf16[256,768]{1,0:T(8,128)(2,1)S(1)}, bf16[256,768]{1,0:T(8,128)(2,1)}, u32[]{:S(2)}) %copy-start) | copy-done | bytes 393240
  2.3 0.2 prep.1.refs_0_.refs_1_
  2.5 3.1 %collective-permute-start.4 = (bf16[264,768]{1,0:T(8,128)(2,1)S(1)}, bf16[264,768]{1,0:T(8,128)(2,1)S(1)}, u32[]{:S(2)}, u32[]{:S(2)}) collective-permute-start(bf16[264,768]{1,0:T(8,128)(2,1)S(1)} %prep.1.refs_0_.refs_1_), channel_id=1, source_target_pairs={{0,8},{1,17},{2,10},{3,19},{4,12},{5,21},{6,14},{7,23},{8,0},{9,25... | collective-permute-start | bytes 1216520 | tf_op jit(solution)/shard_map/ppermute | solution.py:122
  5.6 2.6 %collective-permute-start.6 = (bf16[264,768]{1,0:T(8,128)(2,1)S(1)}, bf16[264,768]{1,0:T(8,128)(2,1)S(1)}, u32[]{:S(2)}, u32[]{:S(2)}) collective-permute-start(bf16[264,768]{1,0:T(8,128)(2,1)S(1)} %prep.1.refs_0_.refs_1_), channel_id=1, source_target_pairs={{0,16},{1,9},{2,18},{3,11},{4,20},{5,13},{6,22},{7,15},{8,24},{9,1... | collective-permute-start | bytes 1216520 | tf_op jit(solution)/shard_map/ppermute | solution.py:122
  8.2 1.5 %collective-permute-start.2 = (bf16[264,768]{1,0:T(8,128)(2,1)S(1)}, bf16[264,768]{1,0:T(8,128)(2,1)S(1)}, u32[]{:S(2)}, u32[]{:S(2)}) collective-permute-start(bf16[264,768]{1,0:T(8,128)(2,1)S(1)} %prep.1.refs_0_.refs_1_), channel_id=1, source_target_pairs={{0,4},{1,5},{2,6},{3,7},{4,0},{5,1},{6,2},{7,3},{8,12},{9,13},{10,... | collective-permute-start | bytes 1216520 | tf_op jit(solution)/shard_map/ppermute | solution.py:122
  9.7 1.5 %collective-permute-start = (bf16[264,768]{1,0:T(8,128)(2,1)S(1)}, bf16[264,768]{1,0:T(8,128)(2,1)S(1)}, u32[]{:S(2)}, u32[]{:S(2)}) collective-permute-start(bf16[264,768]{1,0:T(8,128)(2,1)S(1)} %prep.1.refs_0_.refs_1_), channel_id=1, source_target_pairs={{0,2},{1,3},{2,0},{3,1},{4,6},{5,7},{6,4},{7,5},{8,10},{9,11},{10,... | collective-permute-start | bytes 1216520 | tf_op jit(solution)/shard_map/ppermute | solution.py:122
  11.2 0.0 collective-permute-start.1
  11.2 12.8 %collective-permute-done.4.refs_6_ = bf16[264,768]{1,0:T(8,128)(2,1)S(1)} collective-permute-done((bf16[264,768]{1,0:T(8,128)(2,1)S(1)}, bf16[264,768]{1,0:T(8,128)(2,1)S(1)}, u32[]{:S(2)}, u32[]{:S(2)}) %collective-permute-start.4) | collective-permute-done | bytes 405536 | tf_op jit(solution)/shard_map/ppermute | solution.py:122
  24.0 1.9 %collective-permute-start.5 = (bf16[264,768]{1,0:T(8,128)(2,1)S(1)}, bf16[264,768]{1,0:T(8,128)(2,1)S(1)}, u32[]{:S(2)}, u32[]{:S(2)}) collective-permute-start(bf16[264,768]{1,0:T(8,128)(2,1)S(1)} %collective-permute-done.4.refs_6_), channel_id=1, source_target_pairs={{0,4},{1,3},{2,6},{3,1},{4,0},{5,7},{6,2},{7,5},{8,12},{9,11},{10,... | collective-permute-start | bytes 1216520 | tf_op jit(solution)/shard_map/ppermute | solution.py:122
  25.9 0.0 collective-permute-done.6.refs_8_.refs_3_
  25.9 1.5 %collective-permute-start.10 = (bf16[264,768]{1,0:T(8,128)(2,1)S(1)}, bf16[264,768]{1,0:T(8,128)(2,1)S(1)}, u32[]{:S(2)}, u32[]{:S(2)}) collective-permute-start(bf16[264,768]{1,0:T(8,128)(2,1)S(1)} %collective-permute-done.6.refs_8_.refs_3_), channel_id=1, source_target_pairs={{0,2},{1,5},{2,0},{3,7},{4,6},{5,1},{6,4},{7,3},{8,10},{9,13},{10,... | collective-permute-start | bytes 1216520 | tf_op jit(solution)/shard_map/ppermute | solution.py:122
  27.5 0.0 collective-permute-done.2.refs_3_.refs_4_
  27.5 0.0 collective-permute-start.3
  27.5 0.0 collective-permute-done.refs_1_.refs_2_
  27.5 0.5 collective-permute-start.9
  28.0 0.0 collective-permute-done.1.refs_2_.refs_3_
  28.0 0.1 collective-permute-start.7
  28.1 7.6 %collective-permute-done.5.refs_7_ = bf16[264,768]{1,0:T(8,128)(2,1)S(1)} collective-permute-done((bf16[264,768]{1,0:T(8,128)(2,1)S(1)}, bf16[264,768]{1,0:T(8,128)(2,1)S(1)}, u32[]{:S(2)}, u32[]{:S(2)}) %collective-permute-start.5) | collective-permute-done | bytes 405536 | tf_op jit(solution)/shard_map/ppermute | solution.py:122
  35.7 0.0 collective-permute-start.8
  35.7 0.0 collective-permute-done.10.refs_9_.refs_4_
  35.7 0.5 collective-permute-start.11
  36.2 0.0 collective-permute-done.3.refs_4_.refs_5_
  36.2 1.2 %match.4.refs_0_ = f32[4,256]{1,0:T(4,128)S(1)} custom-call(bf16[264,768]{1,0:T(8,128)(2,1)S(1)} %prep.1.refs_0_.refs_1_, bf16[264,768]{1,0:T(8,128)(2,1)S(1)} %collective-permute-done.refs_1_.refs_2_, bf16[264,768]{1,0:T(8,128)(2,1)S(1)} %collective-permute-done.1.refs_2_.refs_3_, bf16[264,768]{1,0:T(8,128)(2,1)S(1)} %collective-permute-done.2.refs_3_.refs_4_, ...), custom_call_target="tpu_custom_call" | custom-call | flops 805306368 | bytes 1966080 | tf_op jit(solution)/shard_map/match/pallas_call | solution.py:89
  37.3 0.0 collective-permute-done.9.refs_11_.refs_10_
  37.3 0.0 collective-permute-done.7.refs_9_
  37.3 0.0 collective-permute-done.8.refs_10_
  37.4 1.7 %match.5.refs_0_ = f32[4,256]{1,0:T(4,128)S(1)} custom-call(f32[4,256]{1,0:T(4,128)S(1)} %match.4.refs_0_, bf16[264,768]{1,0:T(8,128)(2,1)S(1)} %prep.1.refs_0_.refs_1_, bf16[264,768]{1,0:T(8,128)(2,1)S(1)} %collective-permute-done.refs_1_.refs_2_, bf16[264,768]{1,0:T(8,128)(2,1)S(1)} %collective-permute-done.1.refs_2_.refs_3_, ...), custom_call_target="tpu_custom_call" | custom-call | flops 2013265920 | bytes 4325376 | tf_op jit(solution)/shard_map/match/pallas_call | solution.py:89
  39.1 1.1 %match.6.refs_0_ = f32[4,256]{1,0:T(4,128)S(1)} custom-call(f32[4,256]{1,0:T(4,128)S(1)} %match.5.refs_0_, bf16[264,768]{1,0:T(8,128)(2,1)S(1)} %prep.1.refs_0_.refs_1_, bf16[264,768]{1,0:T(8,128)(2,1)S(1)} %collective-permute-done.refs_1_.refs_2_, bf16[264,768]{1,0:T(8,128)(2,1)S(1)} %collective-permute-done.1.refs_2_.refs_3_, ...), custom_call_target="tpu_custom_call" | custom-call | flops 704643072 | bytes 3932160 | tf_op jit(solution)/shard_map/match/pallas_call | solution.py:89
  40.1 0.0 collective-permute-done.11.refs_5_
  40.2 0.7 %match.7 = f32[4,256]{1,0:T(4,128)S(1)} custom-call(f32[4,256]{1,0:T(4,128)S(1)} %match.6.refs_0_, bf16[264,768]{1,0:T(8,128)(2,1)S(1)} %prep.1.refs_0_.refs_1_, bf16[264,768]{1,0:T(8,128)(2,1)S(1)} %collective-permute-done.refs_1_.refs_2_, bf16[264,768]{1,0:T(8,128)(2,1)S(1)} %collective-permute-done.6.refs_8_.refs_3_, ...), custom_call_target="tpu_custom_call" | custom-call | flops 402653184 | bytes 1966080 | tf_op jit(solution)/shard_map/match/pallas_call | solution.py:89
  40.8 1.0 %collective-permute-start.12 = (f32[4,1,256]{2,0,1:T(4,128)S(1)}, f32[4,1,256]{2,0,1:T(4,128)S(1)}, u32[]{:S(2)}, u32[]{:S(2)}) collective-permute-start(f32[4,1,256]{2,0,1:T(4,128)S(1)} %bitcast.30), channel_id=1, source_target_pairs={{0,16},{1,17},{2,18},{3,19},{4,20},{5,21},{6,22},{7,23},{8,24},{9,... | collective-permute-start | bytes 12296 | tf_op jit(solution)/shard_map/ppermute | solution.py:122
  41.8 3.6 %collective-permute-done.12 = f32[4,1,256]{2,0,1:T(4,128)S(1)} collective-permute-done((f32[4,1,256]{2,0,1:T(4,128)S(1)}, f32[4,1,256]{2,0,1:T(4,128)S(1)}, u32[]{:S(2)}, u32[]{:S(2)}) %collective-permute-start.12) | collective-permute-done | bytes 4128 | tf_op jit(solution)/shard_map/ppermute | solution.py:122
  45.4 0.0 copy-start.4
  45.4 1.8 %collective-permute-start.13 = (f32[4,1,256]{2,0,1:T(4,128)S(1)}, f32[4,1,256]{2,0,1:T(4,128)S(1)}, u32[]{:S(2)}, u32[]{:S(2)}) collective-permute-start(f32[4,1,256]{2,0,1:T(4,128)S(1)} %fusion.2), channel_id=1, source_target_pairs={{0,2},{1,3},{2,0},{3,1},{4,6},{5,7},{6,4},{7,5},{8,10},{9,11},{10,... | collective-permute-start | bytes 12296 | tf_op jit(solution)/shard_map/ppermute | solution.py:122
  47.2 0.0 copy-done.4
  47.9 1.2 %collective-permute-done.13 = f32[4,1,256]{2,0,1:T(4,128)S(1)} collective-permute-done((f32[4,1,256]{2,0,1:T(4,128)S(1)}, f32[4,1,256]{2,0,1:T(4,128)S(1)}, u32[]{:S(2)}, u32[]{:S(2)}) %collective-permute-start.13) | collective-permute-done | bytes 4128 | tf_op jit(solution)/shard_map/ppermute | solution.py:122
  49.1 0.3 fusion
  49.4 0.1 collective-permute-start.14
  49.5 1.1 %collective-permute-done.14 = f32[1,128]{1,0:T(1,128)S(1)} collective-permute-done((f32[1,128]{1,0:T(1,128)S(1)}, f32[1,128]{1,0:T(1,128)S(1)}, u32[]{:S(2)}, u32[]{:S(2)}) %collective-permute-start.14) | collective-permute-done | bytes 544 | tf_op jit(solution)/shard_map/ppermute | solution.py:122
  50.6 1.7 %collective-permute-start.15 = (f32[1,128]{1,0:T(1,128)S(1)}, f32[1,128]{1,0:T(1,128)S(1)}, u32[]{:S(2)}, u32[]{:S(2)}) collective-permute-start(f32[1,128]{1,0:T(1,128)S(1)} %bitcast_add_fusion), channel_id=1, source_target_pairs={{0,4},{1,5},{2,6},{3,7},{4,0},{5,1},{6,2},{7,3},{8,12},{9,13},{10,... | collective-permute-start | bytes 1544 | tf_op jit(solution)/shard_map/ppermute | solution.py:122
  52.4 1.9 %collective-permute-done.15 = f32[1,128]{1,0:T(1,128)S(1)} collective-permute-done((f32[1,128]{1,0:T(1,128)S(1)}, f32[1,128]{1,0:T(1,128)S(1)}, u32[]{:S(2)}, u32[]{:S(2)}) %collective-permute-start.15) | collective-permute-done | bytes 544 | tf_op jit(solution)/shard_map/ppermute | solution.py:122
  54.2 1.2 %collective-permute-start.16 = (f32[1,128]{1,0:T(1,128)S(1)}, f32[1,128]{1,0:T(1,128)S(1)}, u32[]{:S(2)}, u32[]{:S(2)}) collective-permute-start(f32[1,128]{1,0:T(1,128)S(1)} %add.23), channel_id=1, source_target_pairs={{0,8},{1,9},{2,10},{3,11},{4,12},{5,13},{6,14},{7,15},{8,0},{9,1},... | collective-permute-start | bytes 1544 | tf_op jit(solution)/shard_map/ppermute | solution.py:122
  56.1 0.0 copy-start.3
  56.1 1.7 %collective-permute-done.16 = f32[1,128]{1,0:T(1,128)S(1)} collective-permute-done((f32[1,128]{1,0:T(1,128)S(1)}, f32[1,128]{1,0:T(1,128)S(1)}, u32[]{:S(2)}, u32[]{:S(2)}) %collective-permute-start.16) | collective-permute-done | bytes 544 | tf_op jit(solution)/shard_map/ppermute | solution.py:122
  57.8 0.8 %fusion.1 = f32[]{:T(128)} fusion(f32[1,128]{1,0:T(1,128)S(1)} %multiply_subtract_fusion, f32[128]{0:T(128)S(1)} %convert_multiply_fusion, f32[]{:T(128)} %bitcast.12), kind=kLoop, calls=%fused_computation.12 | loop fusion | flops 1015 | bytes 1532 | tf_op jit(solution)/shard_map/reduce_sum | solution.py:224
  59.3 0.0 copy-done.3
  59.3 0.6 add_divide_fusion.1
  (10 shorter events, 0.1 us)
Async XLA Ops:
  0.6 0.7 %copy-start.2 = (s32[256]{0:T(256)S(1)}, s32[256]{0:T(256)}, u32[]{:S(2)}) copy-start(s32[256]{0:T(256)} %param.8) | copy-start | bytes 3076
  0.6 0.7 %copy-start.1 = (s32[256]{0:T(256)S(1)}, s32[256]{0:T(256)}, u32[]{:S(2)}) copy-start(s32[256]{0:T(256)} %param.7) | copy-start | bytes 3076
  1.3 1.0 %copy-start = (bf16[256,768]{1,0:T(8,128)(2,1)S(1)}, bf16[256,768]{1,0:T(8,128)(2,1)}, u32[]{:S(2)}) copy-start(bf16[256,768]{1,0:T(8,128)(2,1)} %rows_ref.1) | copy-start | bytes 1179652
  2.5 21.5 %collective-permute-start.4 = (bf16[264,768]{1,0:T(8,128)(2,1)S(1)}, bf16[264,768]{1,0:T(8,128)(2,1)S(1)}, u32[]{:S(2)}, u32[]{:S(2)}) collective-permute-start(bf16[264,768]{1,0:T(8,128)(2,1)S(1)} %prep.1.refs_0_.refs_1_), channel_id=1, source_target_pairs={{0,8},{1,17},{2,10},{3,19},{4,12},{5,21},{6,14},{7,23},{8,0},{9,25... | collective-permute-start | bytes 1216520 | tf_op jit(solution)/shard_map/ppermute | solution.py:122
  5.6 20.3 %collective-permute-start.6 = (bf16[264,768]{1,0:T(8,128)(2,1)S(1)}, bf16[264,768]{1,0:T(8,128)(2,1)S(1)}, u32[]{:S(2)}, u32[]{:S(2)}) collective-permute-start(bf16[264,768]{1,0:T(8,128)(2,1)S(1)} %prep.1.refs_0_.refs_1_), channel_id=1, source_target_pairs={{0,16},{1,9},{2,18},{3,11},{4,20},{5,13},{6,22},{7,15},{8,24},{9,1... | collective-permute-start | bytes 1216520 | tf_op jit(solution)/shard_map/ppermute | solution.py:122
  8.2 19.3 %collective-permute-start.2 = (bf16[264,768]{1,0:T(8,128)(2,1)S(1)}, bf16[264,768]{1,0:T(8,128)(2,1)S(1)}, u32[]{:S(2)}, u32[]{:S(2)}) collective-permute-start(bf16[264,768]{1,0:T(8,128)(2,1)S(1)} %prep.1.refs_0_.refs_1_), channel_id=1, source_target_pairs={{0,4},{1,5},{2,6},{3,7},{4,0},{5,1},{6,2},{7,3},{8,12},{9,13},{10,... | collective-permute-start | bytes 1216520 | tf_op jit(solution)/shard_map/ppermute | solution.py:122
  9.7 17.8 %collective-permute-start = (bf16[264,768]{1,0:T(8,128)(2,1)S(1)}, bf16[264,768]{1,0:T(8,128)(2,1)S(1)}, u32[]{:S(2)}, u32[]{:S(2)}) collective-permute-start(bf16[264,768]{1,0:T(8,128)(2,1)S(1)} %prep.1.refs_0_.refs_1_), channel_id=1, source_target_pairs={{0,2},{1,3},{2,0},{3,1},{4,6},{5,7},{6,4},{7,5},{8,10},{9,11},{10,... | collective-permute-start | bytes 1216520 | tf_op jit(solution)/shard_map/ppermute | solution.py:122
  11.2 16.8 %collective-permute-start.1 = (bf16[264,768]{1,0:T(8,128)(2,1)S(1)}, bf16[264,768]{1,0:T(8,128)(2,1)S(1)}, u32[]{:S(2)}, u32[]{:S(2)}) collective-permute-start(bf16[264,768]{1,0:T(8,128)(2,1)S(1)} %prep.1.refs_0_.refs_1_), channel_id=1, source_target_pairs={{0,1},{1,0},{2,3},{3,2},{4,5},{5,4},{6,7},{7,6},{8,9},{9,8},{10,11... | collective-permute-start | bytes 1216520 | tf_op jit(solution)/shard_map/ppermute | solution.py:122
  24.0 11.6 %collective-permute-start.5 = (bf16[264,768]{1,0:T(8,128)(2,1)S(1)}, bf16[264,768]{1,0:T(8,128)(2,1)S(1)}, u32[]{:S(2)}, u32[]{:S(2)}) collective-permute-start(bf16[264,768]{1,0:T(8,128)(2,1)S(1)} %collective-permute-done.4.refs_6_), channel_id=1, source_target_pairs={{0,4},{1,3},{2,6},{3,1},{4,0},{5,7},{6,2},{7,5},{8,12},{9,11},{10,... | collective-permute-start | bytes 1216520 | tf_op jit(solution)/shard_map/ppermute | solution.py:122
  25.9 9.7 %collective-permute-start.10 = (bf16[264,768]{1,0:T(8,128)(2,1)S(1)}, bf16[264,768]{1,0:T(8,128)(2,1)S(1)}, u32[]{:S(2)}, u32[]{:S(2)}) collective-permute-start(bf16[264,768]{1,0:T(8,128)(2,1)S(1)} %collective-permute-done.6.refs_8_.refs_3_), channel_id=1, source_target_pairs={{0,2},{1,5},{2,0},{3,7},{4,6},{5,1},{6,4},{7,3},{8,10},{9,13},{10,... | collective-permute-start | bytes 1216520 | tf_op jit(solution)/shard_map/ppermute | solution.py:122
  27.5 8.7 %collective-permute-start.3 = (bf16[264,768]{1,0:T(8,128)(2,1)S(1)}, bf16[264,768]{1,0:T(8,128)(2,1)S(1)}, u32[]{:S(2)}, u32[]{:S(2)}) collective-permute-start(bf16[264,768]{1,0:T(8,128)(2,1)S(1)} %collective-permute-done.2.refs_3_.refs_4_), channel_id=1, source_target_pairs={{0,1},{1,0},{2,3},{3,2},{4,5},{5,4},{6,7},{7,6},{8,9},{9,8},{10,11... | collective-permute-start | bytes 1216520 | tf_op jit(solution)/shard_map/ppermute | solution.py:122
  27.5 9.9 %collective-permute-start.9 = (bf16[264,768]{1,0:T(8,128)(2,1)S(1)}, bf16[264,768]{1,0:T(8,128)(2,1)S(1)}, u32[]{:S(2)}, u32[]{:S(2)}) collective-permute-start(bf16[264,768]{1,0:T(8,128)(2,1)S(1)} %collective-permute-done.6.refs_8_.refs_3_), channel_id=1, source_target_pairs={{0,1},{1,0},{2,3},{3,2},{4,5},{5,4},{6,7},{7,6},{8,9},{9,8},{10,11... | collective-permute-start | bytes 1216520 | tf_op jit(solution)/shard_map/ppermute | solution.py:122
  28.0 9.4 %collective-permute-start.7 = (bf16[264,768]{1,0:T(8,128)(2,1)S(1)}, bf16[264,768]{1,0:T(8,128)(2,1)S(1)}, u32[]{:S(2)}, u32[]{:S(2)}) collective-permute-start(bf16[264,768]{1,0:T(8,128)(2,1)S(1)} %collective-permute-done.4.refs_6_), channel_id=1, source_target_pairs={{0,1},{1,0},{2,3},{3,2},{4,5},{5,4},{6,7},{7,6},{8,9},{9,8},{10,11... | collective-permute-start | bytes 1216520 | tf_op jit(solution)/shard_map/ppermute | solution.py:122
  35.7 1.7 %collective-permute-start.8 = (bf16[264,768]{1,0:T(8,128)(2,1)S(1)}, bf16[264,768]{1,0:T(8,128)(2,1)S(1)}, u32[]{:S(2)}, u32[]{:S(2)}) collective-permute-start(bf16[264,768]{1,0:T(8,128)(2,1)S(1)} %collective-permute-done.5.refs_7_), channel_id=1, source_target_pairs={{0,1},{1,0},{2,3},{3,2},{4,5},{5,4},{6,7},{7,6},{8,9},{9,8},{10,11... | collective-permute-start | bytes 1216520 | tf_op jit(solution)/shard_map/ppermute | solution.py:122
  35.7 4.5 %collective-permute-start.11 = (bf16[264,768]{1,0:T(8,128)(2,1)S(1)}, bf16[264,768]{1,0:T(8,128)(2,1)S(1)}, u32[]{:S(2)}, u32[]{:S(2)}) collective-permute-start(bf16[264,768]{1,0:T(8,128)(2,1)S(1)} %collective-permute-done.10.refs_9_.refs_4_), channel_id=1, source_target_pairs={{0,1},{1,0},{2,3},{3,2},{4,5},{5,4},{6,7},{7,6},{8,9},{9,8},{10,11... | collective-permute-start | bytes 1216520 | tf_op jit(solution)/shard_map/ppermute | solution.py:122
  40.8 4.6 %collective-permute-start.12 = (f32[4,1,256]{2,0,1:T(4,128)S(1)}, f32[4,1,256]{2,0,1:T(4,128)S(1)}, u32[]{:S(2)}, u32[]{:S(2)}) collective-permute-start(f32[4,1,256]{2,0,1:T(4,128)S(1)} %bitcast.30), channel_id=1, source_target_pairs={{0,16},{1,17},{2,18},{3,19},{4,20},{5,21},{6,22},{7,23},{8,24},{9,... | collective-permute-start | bytes 12296 | tf_op jit(solution)/shard_map/ppermute | solution.py:122
  45.4 1.8 %copy-start.4 = (s32[128]{0:T(128)S(1)}, s32[128]{0:T(128)}, u32[]{:S(2)}) copy-start(s32[128]{0:T(128)} %param.9) | copy-start | bytes 1540
  45.4 3.7 %collective-permute-start.13 = (f32[4,1,256]{2,0,1:T(4,128)S(1)}, f32[4,1,256]{2,0,1:T(4,128)S(1)}, u32[]{:S(2)}, u32[]{:S(2)}) collective-permute-start(f32[4,1,256]{2,0,1:T(4,128)S(1)} %fusion.2), channel_id=1, source_target_pairs={{0,2},{1,3},{2,0},{3,1},{4,6},{5,7},{6,4},{7,5},{8,10},{9,11},{10,... | collective-permute-start | bytes 12296 | tf_op jit(solution)/shard_map/ppermute | solution.py:122
  49.4 1.2 %collective-permute-start.14 = (f32[1,128]{1,0:T(1,128)S(1)}, f32[1,128]{1,0:T(1,128)S(1)}, u32[]{:S(2)}, u32[]{:S(2)}) collective-permute-start(f32[1,128]{1,0:T(1,128)S(1)} %bitcast.38), channel_id=1, source_target_pairs={{0,1},{1,0},{2,3},{3,2},{4,5},{5,4},{6,7},{7,6},{8,9},{9,8},{10,11... | collective-permute-start | bytes 1544 | tf_op jit(solution)/shard_map/ppermute | solution.py:122
  50.6 3.6 %collective-permute-start.15 = (f32[1,128]{1,0:T(1,128)S(1)}, f32[1,128]{1,0:T(1,128)S(1)}, u32[]{:S(2)}, u32[]{:S(2)}) collective-permute-start(f32[1,128]{1,0:T(1,128)S(1)} %bitcast_add_fusion), channel_id=1, source_target_pairs={{0,4},{1,5},{2,6},{3,7},{4,0},{5,1},{6,2},{7,3},{8,12},{9,13},{10,... | collective-permute-start | bytes 1544 | tf_op jit(solution)/shard_map/ppermute | solution.py:122
  54.2 3.6 %collective-permute-start.16 = (f32[1,128]{1,0:T(1,128)S(1)}, f32[1,128]{1,0:T(1,128)S(1)}, u32[]{:S(2)}, u32[]{:S(2)}) collective-permute-start(f32[1,128]{1,0:T(1,128)S(1)} %add.23), channel_id=1, source_target_pairs={{0,8},{1,9},{2,10},{3,11},{4,12},{5,13},{6,14},{7,15},{8,0},{9,1},... | collective-permute-start | bytes 1544 | tf_op jit(solution)/shard_map/ppermute | solution.py:122
  56.1 3.2 %copy-start.3 = (f32[1,256]{1,0:T(1,128)}, f32[1,256]{1,0:T(1,128)S(1)}, u32[]{:S(2)}) copy-start(f32[1,256]{1,0:T(1,128)S(1)} %slice.56) | copy-start | bytes 3076
where the time goes:
time: 60.1 us; the launch traced here: 59.9 us
  waiting for transfers between devices  30 us (50%)
  starting transfers between devices  18.9 us (31%)
  Pallas kernels  4.73 us (8%)
  between operations  2.81 us (5%)
  local copies, waits for them, and re-layouts  1.7 us (3%)
  other arithmetic  1.67 us (3%)
    ppermute x17, waiting for transfers between devices, send(): return lax.ppermute(value, AXES, pairs)  30 us
    ppermute x17, starting transfers between devices, send(): return lax.ppermute(value, AXES, pairs)  18.9 us
    pallas_call x4, Pallas kernels, match(): pl.pallas_call(functools.partial(match_kernel, total_docs, docs, plans, s...  4.55 us
    unnamed x11, local copies, waits for them, and re-layouts  1.69 us
  transfers between devices with their start and end apart: 17, of which 7 were waited for; matrix products, arithmetic and copies ran while one was open for 0% of the time, Pallas kernels for 6%

commit v1 on v0

--- a/solution.py
+++ b/solution.py
@@ -15,24 +15,22 @@
     return pl.BlockSpec(memory_space=pltpu.VMEM)
 
 
-def flat_lanes(ref):
-    return jnp.concatenate([ref[i : i + 1, :] for i in range(ref.shape[0])], axis=1)
-
-
-def prep_kernel(rows_ref, label_ref, pos_ref, out_ref):
-    docs, width = rows_ref.shape
+def smem():
+    return pl.BlockSpec(memory_space=pltpu.SMEM)
+
+
+def prep_kernel(rows_ref, key_ref, out_ref):
+    docs = rows_ref.shape[0]
     values = rows_ref[...].astype(jnp.float32)
     total = jnp.sum(values * values, axis=1, keepdims=True)
     out_ref[0:docs, :] = (values / jnp.sqrt(total + 1e-06)).astype(jnp.bfloat16)
-    label = flat_lanes(label_ref)
-    pos = flat_lanes(pos_ref)
-    high = pos >> 8
-    low = pos & 255
-    key = jnp.concatenate([label, high, low], axis=1).astype(jnp.float32)
-    rest = width - key.shape[1]
-    if rest:
-        key = jnp.concatenate([key, jnp.zeros((1, rest), jnp.float32)], axis=1)
-    out_ref[docs:, :] = jnp.broadcast_to(key, (KEY_ROWS, width)).astype(jnp.bfloat16)
+    out_ref[docs:, :] = key_ref[...]
+
+
+def key_rows(label, pos, width):
+    key = jnp.concatenate([label, pos >> 8, pos & 255])
+    key = jnp.pad(key, (0, width - key.shape[0])).astype(jnp.bfloat16)
+    return jnp.broadcast_to(key[None, :], (KEY_ROWS, width))
 
 
 def keys_of(ref, docs, total_docs):
@@ -101,6 +99,27 @@
     )(*args)
 
 
+def sigmoid(x):
+    return 1.0 / (1.0 + jnp.exp(-x))
+
+
+def final_kernel(total_docs, above_ref, other_ref, near_ref, edge_ref, smooth_ref, rate_ref, nearest_ref, keep_ref):
+    bins = edge_ref.shape[1]
+    tau = smooth_ref[0].astype(jnp.float32) / 1000.0
+    rate = rate_ref[0].astype(jnp.float32) / 1000.0
+    edges = edge_ref[...].astype(jnp.float32) / 1000.0
+    step = jnp.concatenate([edges[:, 1:], edges[:, bins - 1 :]], axis=1) - edges
+    below = 1.0 - (above_ref[...] + other_ref[...]) / float(total_docs)
+    cutoff = edges[:, 0:1] + jnp.sum(
+        step * sigmoid((rate - below) / 0.05), axis=1, keepdims=True
+    )
+    near = near_ref[0]
+    keep = sigmoid((cutoff - near) / tau)
+    for i in range(keep_ref.shape[0]):
+        nearest_ref[i : i + 1, :] = near[:, i * 128 : (i + 1) * 128]
+        keep_ref[i : i + 1, :] = keep[:, i * 128 : (i + 1) * 128]
+
+
 def body(
     row_bits,
     col_bits,
@@ -131,23 +150,19 @@
     own = pl.pallas_call(
         prep_kernel,
         out_shape=jax.ShapeDtypeStruct((docs + KEY_ROWS, width), jnp.bfloat16),
-        in_specs=[vmem()] * 3,
+        in_specs=[vmem()] * 2,
         out_specs=vmem(),
         compiler_params=pltpu.CompilerParams(vmem_limit_bytes=24 << 20),
         name="prep",
-    )(
-        document_vectors,
-        group_label.reshape(docs // 128, 128),
-        within_group_position.reshape(docs // 128, 128),
-    )
+    )(document_vectors, key_rows(group_label, within_group_position, width))
     if len(row_bits) == 2 and len(col_bits) == 3:
         far, y = row_bits
         z, x, _ = col_bits
         own_s = swap(own, 1)
-        a1 = split(own, z, far)
+        a1 = split(own, far, z)
         bx = swap(own, x)
         by = swap(own, y)
-        a2 = split(own, far, z)
+        a2 = split(own_s, far ^ 1, z ^ 1)
         bx_s = swap(bx, 1)
         f1 = split(a1, x, y)
         e1 = swap(a1, 1)
@@ -155,40 +170,38 @@
         e2 = swap(a2, 1)
         f2 = split(a2, y, x)
         g2 = swap(f2, 1)
-        row_masks = [0, y, far, y | far]
-        near = match(
-            [own, by, own_s, bx, bx_s],
-            [[(0, [0, 2, 3, 4]), (1, [0, 2, 3, 4]), (0, []), (0, [])]],
-            docs,
-            total_docs,
-        )
-        blocks = [own, by, own_s, bx, bx_s, a1, f1, a2, e1, g1, e2]
+        row_masks = [0, y, far, y ^ far]
+        base = [0, 2, 3, 4]
+        near = match(
+            [own, by, own_s, bx, bx_s], [[(0, base), (1, base), (0, []), (0, [])]], docs, total_docs
+        )
+        blocks = [own, by, own_s, bx, bx_s, a1, e1, f1, g1, a2, e2]
         near = match(
             blocks,
             [
-                [(0, [5, 6, 10]), (1, [5, 6, 10]), (7, [0, 2, 3, 4, 5, 6, 10]), (0, [])],
-                [(0, [7, 8, 9]), (1, [7, 8, 9]), (5, [0, 2, 3, 4, 7, 8, 9]), (6, [0, 2, 3, 4, 7, 8, 9])],
+                [(0, [5, 8, 10]), (1, [5, 8, 10]), (9, base + [5, 8, 10]), (7, base + [5, 8, 10])],
+                [(0, [6, 7, 9]), (1, [6, 7, 9]), (5, base + [6, 7, 9]), (0, [])],
             ],
             docs,
             total_docs,
             near,
         )
-        blocks = [own, by, own_s, bx, bx_s, a1, f1, a2, f2, e2]
+        blocks = [own, by, own_s, bx, bx_s, a1, e1, f1, a2, f2]
         near = match(
             blocks,
             [
-                [(0, []), (0, []), (0, []), (8, [0, 2, 3, 4, 5, 6, 9])],
-                [(0, [8]), (1, [8]), (5, [8]), (6, [8])],
+                [(0, [9]), (1, [9]), (8, [9]), (7, [9])],
+                [(0, []), (0, []), (0, []), (9, base + [6, 7, 8])],
             ],
             docs,
             total_docs,
             near,
         )
         near = match(
-            [own, by, a2, f2, g2],
+            [own, by, a1, f2, g2],
             [
+                [(0, []), (0, []), (0, []), (0, [])],
                 [(0, [4]), (1, [4]), (2, [4]), (3, [4])],
-                [(0, []), (0, []), (0, []), (0, [])],
             ],
             docs,
             total_docs,
@@ -198,9 +211,9 @@
         rows = {0: own}
         cols = {0: own}
         for bit in row_bits:
-            rows.update({mask | bit: swap(block, bit) for mask, block in list(rows.items())})
+            rows.update({mask ^ bit: swap(block, bit) for mask, block in list(rows.items())})
         for bit in col_bits:
-            cols.update({mask | bit: swap(block, bit) for mask, block in list(cols.items())})
+            cols.update({mask ^ bit: swap(block, bit) for mask, block in list(cols.items())})
         row_masks = sorted(rows)
         col_masks = sorted(cols)
         n = len(row_masks)
@@ -213,20 +226,30 @@
         index = [row_masks.index(m ^ bit) for m in row_masks]
         near = jnp.maximum(near, jnp.concatenate([other[i : i + 1] for i in index], axis=0))
     tau = threshold_smoothness[0].astype(jnp.float32) / 1000.0
-    rate = desired_retention_share[0].astype(jnp.float32) / 1000.0
     edges = bucket_boundaries.astype(jnp.float32) / 1000.0
     above = jnp.sum(
         jax.nn.sigmoid((near.reshape(-1)[None, :] - edges[:, None]) / tau), axis=1
     ).reshape(1, bins)
+    other = jnp.zeros_like(above)
     for bit in reversed(col_bits):
-        above = above + swap(above, bit)
-    below = 1.0 - above.reshape(bins) / total_docs
-    cutoff = edges[0] + jnp.sum(
-        (edges[1:] - edges[:-1]) * jax.nn.sigmoid((rate - below[:-1]) / 0.05)
+        above = above + other
+        other = swap(above, bit)
+    nearest, keep = pl.pallas_call(
+        functools.partial(final_kernel, total_docs),
+        out_shape=[jax.ShapeDtypeStruct((docs // 128, 128), jnp.float32)] * 2,
+        in_specs=[vmem()] * 4 + [smem()] * 2,
+        out_specs=[vmem()] * 2,
+        compiler_params=pltpu.CompilerParams(vmem_limit_bytes=24 << 20),
+        name="final",
+    )(
+        above,
+        other,
+        near,
+        bucket_boundaries.reshape(1, bins),
+        threshold_smoothness,
+        desired_retention_share,
     )
-    nearest = near[0].reshape(docs)
-    keep = jax.nn.sigmoid((cutoff - nearest) / tau)
-    return nearest, keep
+    return nearest.reshape(docs), keep.reshape(docs)
 
 
 def solution(mesh):
@@ -235,8 +258,8 @@
     core_bit = 1
     grp_bits = [1 << b for b in range(1, group_size.bit_length() - 1)]
     clu_bits = [group_size << b for b in range(owners.bit_length() - 1)]
-    row_bits = [clu_bits[-1]] + grp_bits
-    col_bits = [clu_bits[-2]] + clu_bits[:-2] + [core_bit]
+    row_bits = [bit | core_bit for bit in [clu_bits[-1]] + grp_bits]
+    col_bits = [bit | core_bit for bit in [clu_bits[-2]] + clu_bits[:-2]] + [core_bit]
     in_specs = (P(AXES, None), P(AXES), P(AXES), P(), P(), P())
     out_specs = (P(AXES), P(AXES))
     return jax.shard_map(

time: 60.1 us -> 56.9 us (0.947)
  waiting for transfers between devices: 30 us -> 29 us
  between operations: 2.81 us -> 2.07 us
  starting transfers between devices: 18.9 us -> 18.2 us
  local copies, waits for them, and re-layouts: 1.7 us -> 1.02 us
  Pallas kernels: 4.73 us -> 5.4 us
  other arithmetic: 1.67 us -> 1.04 us
    ppermute x17, waiting for transfers between devices: 30 us -> 29 us  [send(): return lax.ppermute(value, AXES, pairs)]
    pallas_call x0 -> x1, Pallas kernels: none -> 0.8 us  [body(): pl.pallas_call(functools.partial(final_kernel, total_docs), out_shape=[ja...]
    reduce_sum x1 -> x0, other arithmetic: 0.75 us -> none  [body(): jnp.sum((edges[1:] - edges[:-1]) * jax.nn.sigmoid((rate - below[:-1]) / 0...]
    ppermute x17, starting transfers between devices: 18.9 us -> 18.2 us  [send(): return lax.ppermute(value, AXES, pairs)]
    another operation x0 -> x2, other arithmetic: none -> 0.69 us
    unnamed x11 -> x7, local copies, waits for them, and re-layouts: 1.69 us -> 1 us
  transfers between devices with their start and end apart: 17 -> 17, of which waited for: 7 -> 9; matrix products, arithmetic and copies ran while one was open for 0% -> 0% of each run, Pallas kernels for 6% -> 8%
where the time goes in v1:
time: 56.9 us; the launch traced here: 56.7 us
  waiting for transfers between devices  29 us (51%)
  starting transfers between devices  18.2 us (32%)
  Pallas kernels  5.4 us (9%)
  between operations  2.07 us (4%)
  other arithmetic  1.04 us (2%)
  local copies, waits for them, and re-layouts  1.02 us (2%)
    ppermute x17, waiting for transfers between devices, send(): return lax.ppermute(value, AXES, pairs)  29 us
    ppermute x17, starting transfers between devices, send(): return lax.ppermute(value, AXES, pairs)  18.2 us
    pallas_call x4, Pallas kernels, match(): pl.pallas_call(functools.partial(match_kernel, total_docs, docs, plans, s...  4.42 us
  transfers between devices with their start and end apart: 17, of which 9 were waited for; matrix products, arithmetic and copies ran while one was open for 0% of the time, Pallas kernels for 8%

profile of v1, /device:TPU:0, one launch (start us, length us, event | category | flops | bytes accessed | tf_op | source)
XLA Modules:
  0.0 56.7 jit_solution(9614742292279640056)
XLA Ops:
  0.6 0.0 copy-start.2
  0.6 0.7 %shift-right-arithmetic_convert_fusion = (bf16[256]{0:T(256)(128)(2,1)S(1)}, bf16[256]{0:T(256)(128)(2,1)S(1)}) fusion(s32[256]{0:T(256)} %param.8), kind=kLoop, calls=%fused_computation.12 | loop fusion | flops 1024 | bytes 2048 | tf_op jit(solution)/shard_map/convert.1
  1.3 0.0 copy-done.2
  1.4 0.0 copy-start
  1.4 1.0 %copy-done = bf16[256,768]{1,0:T(8,128)(2,1)S(1)} copy-done((bf16[256,768]{1,0:T(8,128)(2,1)S(1)}, bf16[256,768]{1,0:T(8,128)(2,1)}, u32[]{:S(2)}) %copy-start) | copy-done | bytes 393240
  2.4 0.2 prep.1.refs_0_.refs_1_
  2.5 0.6 collective-permute-start.1
  3.1 3.7 %collective-permute-start.4 = (bf16[264,768]{1,0:T(8,128)(2,1)S(1)}, bf16[264,768]{1,0:T(8,128)(2,1)S(1)}, u32[]{:S(2)}, u32[]{:S(2)}) collective-permute-start(bf16[264,768]{1,0:T(8,128)(2,1)S(1)} %prep.1.refs_0_.refs_1_), channel_id=1, source_target_pairs={{0,17},{1,8},{2,19},{3,10},{4,21},{5,12},{6,23},{7,14},{8,25},{9,0... | collective-permute-start | bytes 1216520 | tf_op jit(solution)/shard_map/ppermute | solution.py:141
  6.8 0.0 collective-permute-done.1.refs_2_.refs_3_
  6.8 1.6 %collective-permute-start.8 = (bf16[264,768]{1,0:T(8,128)(2,1)S(1)}, bf16[264,768]{1,0:T(8,128)(2,1)S(1)}, u32[]{:S(2)}, u32[]{:S(2)}) collective-permute-start(bf16[264,768]{1,0:T(8,128)(2,1)S(1)} %collective-permute-done.1.refs_2_.refs_3_), channel_id=1, source_target_pairs={{0,16},{1,9},{2,18},{3,11},{4,20},{5,13},{6,22},{7,15},{8,24},{9,1... | collective-permute-start | bytes 1216520 | tf_op jit(solution)/shard_map/ppermute | solution.py:141
  8.4 0.0 collective-permute-start.2
  8.4 8.1 %collective-permute-done.4.refs_6_.refs_3_ = bf16[264,768]{1,0:T(8,128)(2,1)S(1)} collective-permute-done((bf16[264,768]{1,0:T(8,128)(2,1)S(1)}, bf16[264,768]{1,0:T(8,128)(2,1)S(1)}, u32[]{:S(2)}, u32[]{:S(2)}) %collective-permute-start.4) | collective-permute-done | bytes 405536 | tf_op jit(solution)/shard_map/ppermute | solution.py:141
  16.6 0.8 %collective-permute-start.6 = (bf16[264,768]{1,0:T(8,128)(2,1)S(1)}, bf16[264,768]{1,0:T(8,128)(2,1)S(1)}, u32[]{:S(2)}, u32[]{:S(2)}) collective-permute-start(bf16[264,768]{1,0:T(8,128)(2,1)S(1)} %collective-permute-done.4.refs_6_.refs_3_), channel_id=1, source_target_pairs={{0,5},{1,2},{2,7},{3,0},{4,1},{5,6},{6,3},{7,4},{8,13},{9,10},{10,... | collective-permute-start | bytes 1216520 | tf_op jit(solution)/shard_map/ppermute | solution.py:141
  17.4 1.0 %collective-permute-start = (bf16[264,768]{1,0:T(8,128)(2,1)S(1)}, bf16[264,768]{1,0:T(8,128)(2,1)S(1)}, u32[]{:S(2)}, u32[]{:S(2)}) collective-permute-start(bf16[264,768]{1,0:T(8,128)(2,1)S(1)} %prep.1.refs_0_.refs_1_), channel_id=1, source_target_pairs={{0,3},{1,2},{2,1},{3,0},{4,7},{5,6},{6,5},{7,4},{8,11},{9,10},{10,... | collective-permute-start | bytes 1216520 | tf_op jit(solution)/shard_map/ppermute | solution.py:141
  18.3 6.1 %collective-permute-done.8.refs_10_.refs_9_ = bf16[264,768]{1,0:T(8,128)(2,1)S(1)} collective-permute-done((bf16[264,768]{1,0:T(8,128)(2,1)S(1)}, bf16[264,768]{1,0:T(8,128)(2,1)S(1)}, u32[]{:S(2)}, u32[]{:S(2)}) %collective-permute-start.8) | collective-permute-done | bytes 405536 | tf_op jit(solution)/shard_map/ppermute | solution.py:141
  24.4 0.8 %collective-permute-start.10 = (bf16[264,768]{1,0:T(8,128)(2,1)S(1)}, bf16[264,768]{1,0:T(8,128)(2,1)S(1)}, u32[]{:S(2)}, u32[]{:S(2)}) collective-permute-start(bf16[264,768]{1,0:T(8,128)(2,1)S(1)} %collective-permute-done.8.refs_10_.refs_9_), channel_id=1, source_target_pairs={{0,3},{1,4},{2,1},{3,6},{4,7},{5,0},{6,5},{7,2},{8,11},{9,12},{10,... | collective-permute-start | bytes 1216520 | tf_op jit(solution)/shard_map/ppermute | solution.py:141
  25.2 0.0 collective-permute-done.2.refs_3_.refs_4_
  25.2 1.6 %collective-permute-start.3 = (bf16[264,768]{1,0:T(8,128)(2,1)S(1)}, bf16[264,768]{1,0:T(8,128)(2,1)S(1)}, u32[]{:S(2)}, u32[]{:S(2)}) collective-permute-start(bf16[264,768]{1,0:T(8,128)(2,1)S(1)} %collective-permute-done.2.refs_3_.refs_4_), channel_id=1, source_target_pairs={{0,1},{1,0},{2,3},{3,2},{4,5},{5,4},{6,7},{7,6},{8,9},{9,8},{10,11... | collective-permute-start | bytes 1216520 | tf_op jit(solution)/shard_map/ppermute | solution.py:141
  26.7 0.0 collective-permute-start.5
  26.7 0.0 collective-permute-done.6.refs_8_
  26.7 0.5 collective-permute-start.7
  27.2 7.9 %collective-permute-done.refs_1_.refs_2_ = bf16[264,768]{1,0:T(8,128)(2,1)S(1)} collective-permute-done((bf16[264,768]{1,0:T(8,128)(2,1)S(1)}, bf16[264,768]{1,0:T(8,128)(2,1)S(1)}, u32[]{:S(2)}, u32[]{:S(2)}) %collective-permute-start) | collective-permute-done | bytes 405536 | tf_op jit(solution)/shard_map/ppermute | solution.py:141
  35.1 0.2 collective-permute-start.9
  35.3 0.7 %collective-permute-done.10.refs_10_.refs_4_ = bf16[264,768]{1,0:T(8,128)(2,1)S(1)} collective-permute-done((bf16[264,768]{1,0:T(8,128)(2,1)S(1)}, bf16[264,768]{1,0:T(8,128)(2,1)S(1)}, u32[]{:S(2)}, u32[]{:S(2)}) %collective-permute-start.10) | collective-permute-done | bytes 405536 | tf_op jit(solution)/shard_map/ppermute | solution.py:141
  36.0 0.8 %collective-permute-start.11 = (bf16[264,768]{1,0:T(8,128)(2,1)S(1)}, bf16[264,768]{1,0:T(8,128)(2,1)S(1)}, u32[]{:S(2)}, u32[]{:S(2)}) collective-permute-start(bf16[264,768]{1,0:T(8,128)(2,1)S(1)} %collective-permute-done.10.refs_10_.refs_4_), channel_id=1, source_target_pairs={{0,1},{1,0},{2,3},{3,2},{4,5},{5,4},{6,7},{7,6},{8,9},{9,8},{10,11... | collective-permute-start | bytes 1216520 | tf_op jit(solution)/shard_map/ppermute | solution.py:141
  36.8 0.0 collective-permute-done.3.refs_4_.refs_5_
  36.8 1.2 %match.4.refs_0_ = f32[4,256]{1,0:T(4,128)S(1)} custom-call(bf16[264,768]{1,0:T(8,128)(2,1)S(1)} %prep.1.refs_0_.refs_1_, bf16[264,768]{1,0:T(8,128)(2,1)S(1)} %collective-permute-done.refs_1_.refs_2_, bf16[264,768]{1,0:T(8,128)(2,1)S(1)} %collective-permute-done.1.refs_2_.refs_3_, bf16[264,768]{1,0:T(8,128)(2,1)S(1)} %collective-permute-done.2.refs_3_.refs_4_, ...), custom_call_target="tpu_custom_call" | custom-call | flops 805306368 | bytes 1966080 | tf_op jit(solution)/shard_map/match/pallas_call | solution.py:87
  37.9 0.0 collective-permute-done.5.refs_7_
  37.9 0.0 collective-permute-done.7.refs_9_
  38.0 0.0 collective-permute-done.9.refs_11_
  38.0 2.6 %match.5.refs_0_ = f32[4,256]{1,0:T(4,128)S(1)} custom-call(f32[4,256]{1,0:T(4,128)S(1)} %match.4.refs_0_, bf16[264,768]{1,0:T(8,128)(2,1)S(1)} %prep.1.refs_0_.refs_1_, bf16[264,768]{1,0:T(8,128)(2,1)S(1)} %collective-permute-done.refs_1_.refs_2_, bf16[264,768]{1,0:T(8,128)(2,1)S(1)} %collective-permute-done.1.refs_2_.refs_3_, ...), custom_call_target="tpu_custom_call" | custom-call | flops 2013265920 | bytes 4325376 | tf_op jit(solution)/shard_map/match/pallas_call | solution.py:87
  40.5 0.7 %match.6.refs_0_ = f32[4,256]{1,0:T(4,128)S(1)} custom-call(f32[4,256]{1,0:T(4,128)S(1)} %match.5.refs_0_, bf16[264,768]{1,0:T(8,128)(2,1)S(1)} %prep.1.refs_0_.refs_1_, bf16[264,768]{1,0:T(8,128)(2,1)S(1)} %collective-permute-done.refs_1_.refs_2_, bf16[264,768]{1,0:T(8,128)(2,1)S(1)} %collective-permute-done.1.refs_2_.refs_3_, ...), custom_call_target="tpu_custom_call" | custom-call | flops 704643072 | bytes 3932160 | tf_op jit(solution)/shard_map/match/pallas_call | solution.py:87
  41.2 0.0 collective-permute-done.11.refs_5_
  41.3 2.5 %collective-permute-start.12 = (f32[4,1,256]{2,0,1:T(4,128)S(1)}, f32[4,1,256]{2,0,1:T(4,128)S(1)}, u32[]{:S(2)}, u32[]{:S(2)}) collective-permute-start(f32[4,1,256]{2,0,1:T(4,128)S(1)} %bitcast.23), channel_id=1, source_target_pairs={{0,17},{1,16},{2,19},{3,18},{4,21},{5,20},{6,23},{7,22},{8,25},{9,... | collective-permute-start | bytes 12296 | tf_op jit(solution)/shard_map/ppermute | solution.py:141
  43.7 1.5 %collective-permute-done.12 = f32[4,1,256]{2,0,1:T(4,128)S(1)} collective-permute-done((f32[4,1,256]{2,0,1:T(4,128)S(1)}, f32[4,1,256]{2,0,1:T(4,128)S(1)}, u32[]{:S(2)}, u32[]{:S(2)}) %collective-permute-start.12) | collective-permute-done | bytes 4128 | tf_op jit(solution)/shard_map/ppermute | solution.py:141
  45.3 0.0 copy-start.1
  45.3 1.4 %collective-permute-start.13 = (f32[4,1,256]{2,0,1:T(4,128)S(1)}, f32[4,1,256]{2,0,1:T(4,128)S(1)}, u32[]{:S(2)}, u32[]{:S(2)}) collective-permute-start(f32[4,1,256]{2,0,1:T(4,128)S(1)} %fusion.1), channel_id=1, source_target_pairs={{0,3},{1,2},{2,1},{3,0},{4,7},{5,6},{6,5},{7,4},{8,11},{9,10},{10,... | collective-permute-start | bytes 12296 | tf_op jit(solution)/shard_map/ppermute | solution.py:141
  46.7 0.0 copy-done.1
  47.3 1.0 %collective-permute-done.13 = f32[4,1,256]{2,0,1:T(4,128)S(1)} collective-permute-done((f32[4,1,256]{2,0,1:T(4,128)S(1)}, f32[4,1,256]{2,0,1:T(4,128)S(1)}, u32[]{:S(2)}, u32[]{:S(2)}) %collective-permute-start.13) | collective-permute-done | bytes 4128 | tf_op jit(solution)/shard_map/ppermute | solution.py:141
  48.4 0.3 fusion
  48.7 0.3 collective-permute-start.14
  49.0 1.0 %collective-permute-done.14 = f32[1,128]{1,0:T(1,128)S(1)} collective-permute-done((f32[1,128]{1,0:T(1,128)S(1)}, f32[1,128]{1,0:T(1,128)S(1)}, u32[]{:S(2)}, u32[]{:S(2)}) %collective-permute-start.14) | collective-permute-done | bytes 544 | tf_op jit(solution)/shard_map/ppermute | solution.py:141
  49.9 1.3 %collective-permute-start.15 = (f32[1,128]{1,0:T(1,128)S(1)}, f32[1,128]{1,0:T(1,128)S(1)}, u32[]{:S(2)}, u32[]{:S(2)}) collective-permute-start(f32[1,128]{1,0:T(1,128)S(1)} %bitcast_add_fusion), channel_id=1, source_target_pairs={{0,5},{1,4},{2,7},{3,6},{4,1},{5,0},{6,3},{7,2},{8,13},{9,12},{10,... | collective-permute-start | bytes 1544 | tf_op jit(solution)/shard_map/ppermute | solution.py:141
  51.2 1.7 %collective-permute-done.15 = f32[1,128]{1,0:T(1,128)S(1)} collective-permute-done((f32[1,128]{1,0:T(1,128)S(1)}, f32[1,128]{1,0:T(1,128)S(1)}, u32[]{:S(2)}, u32[]{:S(2)}) %collective-permute-start.15) | collective-permute-done | bytes 544 | tf_op jit(solution)/shard_map/ppermute | solution.py:141
  52.9 1.4 %collective-permute-start.16 = (f32[1,128]{1,0:T(1,128)S(1)}, f32[1,128]{1,0:T(1,128)S(1)}, u32[]{:S(2)}, u32[]{:S(2)}) collective-permute-start(f32[1,128]{1,0:T(1,128)S(1)} %add.11.above_ref), channel_id=1, source_target_pairs={{0,9},{1,8},{2,11},{3,10},{4,13},{5,12},{6,15},{7,14},{8,1},{9,0},... | collective-permute-start | bytes 1544 | tf_op jit(solution)/shard_map/ppermute | solution.py:141
  55.0 1.0 %collective-permute-done.16.other_ref = f32[1,128]{1,0:T(1,128)S(1)} collective-permute-done((f32[1,128]{1,0:T(1,128)S(1)}, f32[1,128]{1,0:T(1,128)S(1)}, u32[]{:S(2)}, u32[]{:S(2)}) %collective-permute-start.16) | collective-permute-done | bytes 544 | tf_op jit(solution)/shard_map/ppermute | solution.py:141
  55.9 0.8 %final.1 = (f32[2,128]{1,0:T(2,128)}, f32[2,128]{1,0:T(2,128)}) custom-call(f32[1,128]{1,0:T(1,128)S(1)} %add.11.above_ref, f32[1,128]{1,0:T(1,128)S(1)} %collective-permute-done.16.other_ref, f32[4,1,256]{2,1,0:T(1,128)S(1)} %max.14.near_ref, s32[1,128]{1,0:T(1,128)S(1)} %bitcast.24, s32[1]{0:T(128)S(6)} %copy.9.smooth_ref, s32[1]{0:T(128)S(6)} %copy.10.rate_ref), custom_call_target="tpu_custom_call" | custom-call | tf_op jit(solution)/shard_map/final/pallas_call | solution.py:237
  (13 shorter events, 0.1 us)
Async XLA Ops:
  0.6 0.7 %copy-start.2 = (s32[256]{0:T(256)S(1)}, s32[256]{0:T(256)}, u32[]{:S(2)}) copy-start(s32[256]{0:T(256)} %param.7) | copy-start | bytes 3076
  1.4 1.0 %copy-start = (bf16[256,768]{1,0:T(8,128)(2,1)S(1)}, bf16[256,768]{1,0:T(8,128)(2,1)}, u32[]{:S(2)}) copy-start(bf16[256,768]{1,0:T(8,128)(2,1)} %rows_ref.1) | copy-start | bytes 1179652
  2.5 4.2 %collective-permute-start.1 = (bf16[264,768]{1,0:T(8,128)(2,1)S(1)}, bf16[264,768]{1,0:T(8,128)(2,1)S(1)}, u32[]{:S(2)}, u32[]{:S(2)}) collective-permute-start(bf16[264,768]{1,0:T(8,128)(2,1)S(1)} %prep.1.refs_0_.refs_1_), channel_id=1, source_target_pairs={{0,1},{1,0},{2,3},{3,2},{4,5},{5,4},{6,7},{7,6},{8,9},{9,8},{10,11... | collective-permute-start | bytes 1216520 | tf_op jit(solution)/shard_map/ppermute | solution.py:141
  3.1 13.5 %collective-permute-start.4 = (bf16[264,768]{1,0:T(8,128)(2,1)S(1)}, bf16[264,768]{1,0:T(8,128)(2,1)S(1)}, u32[]{:S(2)}, u32[]{:S(2)}) collective-permute-start(bf16[264,768]{1,0:T(8,128)(2,1)S(1)} %prep.1.refs_0_.refs_1_), channel_id=1, source_target_pairs={{0,17},{1,8},{2,19},{3,10},{4,21},{5,12},{6,23},{7,14},{8,25},{9,0... | collective-permute-start | bytes 1216520 | tf_op jit(solution)/shard_map/ppermute | solution.py:141
  6.8 17.6 %collective-permute-start.8 = (bf16[264,768]{1,0:T(8,128)(2,1)S(1)}, bf16[264,768]{1,0:T(8,128)(2,1)S(1)}, u32[]{:S(2)}, u32[]{:S(2)}) collective-permute-start(bf16[264,768]{1,0:T(8,128)(2,1)S(1)} %collective-permute-done.1.refs_2_.refs_3_), channel_id=1, source_target_pairs={{0,16},{1,9},{2,18},{3,11},{4,20},{5,13},{6,22},{7,15},{8,24},{9,1... | collective-permute-start | bytes 1216520 | tf_op jit(solution)/shard_map/ppermute | solution.py:141
  8.4 16.7 %collective-permute-start.2 = (bf16[264,768]{1,0:T(8,128)(2,1)S(1)}, bf16[264,768]{1,0:T(8,128)(2,1)S(1)}, u32[]{:S(2)}, u32[]{:S(2)}) collective-permute-start(bf16[264,768]{1,0:T(8,128)(2,1)S(1)} %prep.1.refs_0_.refs_1_), channel_id=1, source_target_pairs={{0,5},{1,4},{2,7},{3,6},{4,1},{5,0},{6,3},{7,2},{8,13},{9,12},{10,... | collective-permute-start | bytes 1216520 | tf_op jit(solution)/shard_map/ppermute | solution.py:141
  16.6 10.2 %collective-permute-start.6 = (bf16[264,768]{1,0:T(8,128)(2,1)S(1)}, bf16[264,768]{1,0:T(8,128)(2,1)S(1)}, u32[]{:S(2)}, u32[]{:S(2)}) collective-permute-start(bf16[264,768]{1,0:T(8,128)(2,1)S(1)} %collective-permute-done.4.refs_6_.refs_3_), channel_id=1, source_target_pairs={{0,5},{1,2},{2,7},{3,0},{4,1},{5,6},{6,3},{7,4},{8,13},{9,10},{10,... | collective-permute-start | bytes 1216520 | tf_op jit(solution)/shard_map/ppermute | solution.py:141
  17.4 17.8 %collective-permute-start = (bf16[264,768]{1,0:T(8,128)(2,1)S(1)}, bf16[264,768]{1,0:T(8,128)(2,1)S(1)}, u32[]{:S(2)}, u32[]{:S(2)}) collective-permute-start(bf16[264,768]{1,0:T(8,128)(2,1)S(1)} %prep.1.refs_0_.refs_1_), channel_id=1, source_target_pairs={{0,3},{1,2},{2,1},{3,0},{4,7},{5,6},{6,5},{7,4},{8,11},{9,10},{10,... | collective-permute-start | bytes 1216520 | tf_op jit(solution)/shard_map/ppermute | solution.py:141
  24.4 11.6 %collective-permute-start.10 = (bf16[264,768]{1,0:T(8,128)(2,1)S(1)}, bf16[264,768]{1,0:T(8,128)(2,1)S(1)}, u32[]{:S(2)}, u32[]{:S(2)}) collective-permute-start(bf16[264,768]{1,0:T(8,128)(2,1)S(1)} %collective-permute-done.8.refs_10_.refs_9_), channel_id=1, source_target_pairs={{0,3},{1,4},{2,1},{3,6},{4,7},{5,0},{6,5},{7,2},{8,11},{9,12},{10,... | collective-permute-start | bytes 1216520 | tf_op jit(solution)/shard_map/ppermute | solution.py:141
  25.2 11.6 %collective-permute-start.3 = (bf16[264,768]{1,0:T(8,128)(2,1)S(1)}, bf16[264,768]{1,0:T(8,128)(2,1)S(1)}, u32[]{:S(2)}, u32[]{:S(2)}) collective-permute-start(bf16[264,768]{1,0:T(8,128)(2,1)S(1)} %collective-permute-done.2.refs_3_.refs_4_), channel_id=1, source_target_pairs={{0,1},{1,0},{2,3},{3,2},{4,5},{5,4},{6,7},{7,6},{8,9},{9,8},{10,11... | collective-permute-start | bytes 1216520 | tf_op jit(solution)/shard_map/ppermute | solution.py:141
  26.7 11.2 %collective-permute-start.5 = (bf16[264,768]{1,0:T(8,128)(2,1)S(1)}, bf16[264,768]{1,0:T(8,128)(2,1)S(1)}, u32[]{:S(2)}, u32[]{:S(2)}) collective-permute-start(bf16[264,768]{1,0:T(8,128)(2,1)S(1)} %collective-permute-done.4.refs_6_.refs_3_), channel_id=1, source_target_pairs={{0,1},{1,0},{2,3},{3,2},{4,5},{5,4},{6,7},{7,6},{8,9},{9,8},{10,11... | collective-permute-start | bytes 1216520 | tf_op jit(solution)/shard_map/ppermute | solution.py:141
  26.7 11.2 %collective-permute-start.7 = (bf16[264,768]{1,0:T(8,128)(2,1)S(1)}, bf16[264,768]{1,0:T(8,128)(2,1)S(1)}, u32[]{:S(2)}, u32[]{:S(2)}) collective-permute-start(bf16[264,768]{1,0:T(8,128)(2,1)S(1)} %collective-permute-done.6.refs_8_), channel_id=1, source_target_pairs={{0,1},{1,0},{2,3},{3,2},{4,5},{5,4},{6,7},{7,6},{8,9},{9,8},{10,11... | collective-permute-start | bytes 1216520 | tf_op jit(solution)/shard_map/ppermute | solution.py:141
  35.1 2.8 %collective-permute-start.9 = (bf16[264,768]{1,0:T(8,128)(2,1)S(1)}, bf16[264,768]{1,0:T(8,128)(2,1)S(1)}, u32[]{:S(2)}, u32[]{:S(2)}) collective-permute-start(bf16[264,768]{1,0:T(8,128)(2,1)S(1)} %collective-permute-done.8.refs_10_.refs_9_), channel_id=1, source_target_pairs={{0,1},{1,0},{2,3},{3,2},{4,5},{5,4},{6,7},{7,6},{8,9},{9,8},{10,11... | collective-permute-start | bytes 1216520 | tf_op jit(solution)/shard_map/ppermute | solution.py:141
  36.0 5.2 %collective-permute-start.11 = (bf16[264,768]{1,0:T(8,128)(2,1)S(1)}, bf16[264,768]{1,0:T(8,128)(2,1)S(1)}, u32[]{:S(2)}, u32[]{:S(2)}) collective-permute-start(bf16[264,768]{1,0:T(8,128)(2,1)S(1)} %collective-permute-done.10.refs_10_.refs_4_), channel_id=1, source_target_pairs={{0,1},{1,0},{2,3},{3,2},{4,5},{5,4},{6,7},{7,6},{8,9},{9,8},{10,11... | collective-permute-start | bytes 1216520 | tf_op jit(solution)/shard_map/ppermute | solution.py:141
  41.3 4.0 %collective-permute-start.12 = (f32[4,1,256]{2,0,1:T(4,128)S(1)}, f32[4,1,256]{2,0,1:T(4,128)S(1)}, u32[]{:S(2)}, u32[]{:S(2)}) collective-permute-start(f32[4,1,256]{2,0,1:T(4,128)S(1)} %bitcast.23), channel_id=1, source_target_pairs={{0,17},{1,16},{2,19},{3,18},{4,21},{5,20},{6,23},{7,22},{8,25},{9,... | collective-permute-start | bytes 12296 | tf_op jit(solution)/shard_map/ppermute | solution.py:141
  45.3 1.4 %copy-start.1 = (s32[128]{0:T(128)S(1)}, s32[128]{0:T(128)}, u32[]{:S(2)}) copy-start(s32[128]{0:T(128)} %param.9) | copy-start | bytes 1540
  45.3 3.1 %collective-permute-start.13 = (f32[4,1,256]{2,0,1:T(4,128)S(1)}, f32[4,1,256]{2,0,1:T(4,128)S(1)}, u32[]{:S(2)}, u32[]{:S(2)}) collective-permute-start(f32[4,1,256]{2,0,1:T(4,128)S(1)} %fusion.1), channel_id=1, source_target_pairs={{0,3},{1,2},{2,1},{3,0},{4,7},{5,6},{6,5},{7,4},{8,11},{9,10},{10,... | collective-permute-start | bytes 12296 | tf_op jit(solution)/shard_map/ppermute | solution.py:141
  48.7 1.2 %collective-permute-start.14 = (f32[1,128]{1,0:T(1,128)S(1)}, f32[1,128]{1,0:T(1,128)S(1)}, u32[]{:S(2)}, u32[]{:S(2)}) collective-permute-start(f32[1,128]{1,0:T(1,128)S(1)} %bitcast.29), channel_id=1, source_target_pairs={{0,1},{1,0},{2,3},{3,2},{4,5},{5,4},{6,7},{7,6},{8,9},{9,8},{10,11... | collective-permute-start | bytes 1544 | tf_op jit(solution)/shard_map/ppermute | solution.py:141
  49.9 3.0 %collective-permute-start.15 = (f32[1,128]{1,0:T(1,128)S(1)}, f32[1,128]{1,0:T(1,128)S(1)}, u32[]{:S(2)}, u32[]{:S(2)}) collective-permute-start(f32[1,128]{1,0:T(1,128)S(1)} %bitcast_add_fusion), channel_id=1, source_target_pairs={{0,5},{1,4},{2,7},{3,6},{4,1},{5,0},{6,3},{7,2},{8,13},{9,12},{10,... | collective-permute-start | bytes 1544 | tf_op jit(solution)/shard_map/ppermute | solution.py:141
  52.9 3.0 %collective-permute-start.16 = (f32[1,128]{1,0:T(1,128)S(1)}, f32[1,128]{1,0:T(1,128)S(1)}, u32[]{:S(2)}, u32[]{:S(2)}) collective-permute-start(f32[1,128]{1,0:T(1,128)S(1)} %add.11.above_ref), channel_id=1, source_target_pairs={{0,9},{1,8},{2,11},{3,10},{4,13},{5,12},{6,15},{7,14},{8,1},{9,0},... | collective-permute-start | bytes 1544 | tf_op jit(solution)/shard_map/ppermute | solution.py:141
